TPU v7x, 32 devices: a whole 2x2x4 slice. The times are simulated.
32 devices in a mesh: fsdp: 8 (over y, x, core), cp: 4 (over z).
Axes of the slice: x: 2, y: 2, z: 4, core: 2. Of those that a mesh axis runs over, the one named last changes fastest.
Arguments:
- features: bfloat16 [8, 512, 2560], P('fsdp', 'cp'), may hold values from -6 to 6
- query_rows: bfloat16 [8, 512, 1280], P('fsdp', 'cp'), may hold values from -40 to 40, as said below
- key_rows: bfloat16 [8, 512, 1280], P('fsdp', 'cp'), may hold values from -4 to 4
- value_rows: bfloat16 [8, 512, 1280], P('fsdp', 'cp'), may hold values from -6 to 6
- attn_output: bfloat16 [8, 512, 1280], P('fsdp', 'cp'), may hold values from -6 to 6
- grad_output: bfloat16 [8, 512, 1280], P('fsdp', 'cp'), may hold values from -6 to 6
- log_sums: float32 [8, 512, 10], P('fsdp', 'cp'), as said below
Outputs:
- d_query: bfloat16 [8, 512, 1280], P('fsdp', 'cp')
- d_key: bfloat16 [8, 512, 1280], P('fsdp', 'cp')
- d_value: bfloat16 [8, 512, 1280], P('fsdp', 'cp')
- d_value_weight: float32 [2560, 1280], P('fsdp', 'cp')
Inputs may be any that keep to these rules, and one draw needn't show every extreme that they name: `query_rows`: queries of a clip, with key_rows and log_sums drawn together with them. log_sums[c, t, h] is the logarithm of the sum over all 512 keys u of clip c of exp(128**-0.5 * q[t] . k[u]) for head h, computed from the bfloat16 queries and keys in float32.
All inputs are finite; a program needn't handle non-finite values.
Results may differ from a plain program's by a relative error of at most 0.02.
Values may be sent and summed in bfloat16 or wider, within the bound.
No kernel may reach another device: no remote copies, remote signals or barrier semaphores. Data moves between devices by JAX's collectives and lax.ppermute only.
A program may use at most 128 MiB of HBM per device.

v0:
```python
import jax
import jax.numpy as jnp
from jax import lax
from jax.sharding import PartitionSpec as P


def passed_along(value, axis, steps):
    count = lax.axis_size(axis)
    pairs = [(source, (source + steps) % count) for source in range(count)]
    return lax.ppermute(value, axis, pairs)


def on_device(features, query_rows, key_rows, value_rows, attn_output, grad_output, log_sums):
    rows_here = query_rows.shape[1]
    proj_width = query_rows.shape[2]
    head_count = log_sums.shape[2]
    head_size = proj_width // head_count
    softmax_scale = head_size ** (-0.5)

    def as_heads(block):
        return block[0].reshape(block.shape[1], head_count, head_size)

    product = grad_output.astype(jnp.float32) * attn_output.astype(jnp.float32)
    row_delta = jnp.sum(product.reshape(1, rows_here, head_count, head_size), axis=3)
    own_key = as_heads(key_rows)
    own_value = as_heads(value_rows)
    all_norms, all_deltas = (
        lax.all_gather(log_sums, "cp", axis=1, tiled=True),
        lax.all_gather(row_delta, "cp", axis=1, tiled=True),
    )

    def pair_scores(query_heads, grad_heads, offset, rows_in):
        norm_block = lax.dynamic_slice_in_dim(all_norms, offset, rows_in, 1)[0].T
        delta_block = lax.dynamic_slice_in_dim(all_deltas, offset, rows_in, 1)[0].T
        scores = (
            jnp.einsum("qhd,khd->hqk", query_heads, own_key, preferred_element_type=jnp.float32)
            * softmax_scale
        )
        attn_prob = jnp.exp(scores - norm_block[:, :, None])
        grad_prob = jnp.einsum(
            "qhd,khd->hqk", grad_heads, own_value, preferred_element_type=jnp.float32
        )
        grad_score = (attn_prob * (grad_prob - delta_block[:, :, None])).astype(jnp.bfloat16)
        return (grad_score, attn_prob.astype(jnp.bfloat16))

    zero_rows = jnp.zeros((rows_here, head_count, head_size), jnp.float32)
    position = lax.axis_index("cp")
    cycle_count = lax.axis_size("cp")

    def cycle_step(step, state):
        query_block, grad_block, query_run, key_run, value_run = state
        source = (position - step) % cycle_count
        offset = source * rows_here
        query_heads = as_heads(query_block)
        grad_heads = as_heads(grad_block)
        grad_score, prob_half = pair_scores(query_heads, grad_heads, offset, rows_here)
        query_run = query_run + jnp.einsum(
            "hqk,khd->qhd", grad_score, own_key, preferred_element_type=jnp.float32
        )
        key_run = key_run + jnp.einsum(
            "hqk,qhd->khd", grad_score, query_heads, preferred_element_type=jnp.float32
        )
        value_run = value_run + jnp.einsum(
            "hqk,qhd->khd", prob_half, grad_heads, preferred_element_type=jnp.float32
        )
        query_block, grad_block = passed_along((query_block, grad_block), "cp", 1)
        query_run = passed_along(query_run.astype(jnp.bfloat16), "cp", 1).astype(query_run.dtype)
        return (query_block, grad_block, query_run, key_run, value_run)

    start_state = (query_rows, grad_output, zero_rows, zero_rows, zero_rows)
    final_state = lax.fori_loop(0, cycle_count, cycle_step, start_state)
    query_total, key_total, value_total = (final_state[2], final_state[3], final_state[4])
    d_query = (softmax_scale * query_total).astype(jnp.bfloat16).reshape(1, rows_here, proj_width)
    d_key = (softmax_scale * key_total).astype(jnp.bfloat16).reshape(1, rows_here, proj_width)
    d_value = value_total.astype(jnp.bfloat16).reshape(1, rows_here, proj_width)
    feature_cols = features[0]
    row_sums = lax.psum_scatter(
        jnp.einsum(
            "tf,tw->fw", feature_cols, d_value[0], preferred_element_type=jnp.float32
        ).astype(jnp.bfloat16),
        "fsdp",
        scatter_dimension=0,
        tiled=True,
    )
    weight_part = lax.psum_scatter(row_sums, "cp", scatter_dimension=1, tiled=True).astype(
        jnp.float32
    )
    return (d_query, d_key, d_value, weight_part)


def solution(mesh):
    return jax.shard_map(
        on_device,
        mesh=mesh,
        in_specs=(
            P("fsdp", "cp", None),
            P("fsdp", "cp", None),
            P("fsdp", "cp", None),
            P("fsdp", "cp", None),
            P("fsdp", "cp", None),
            P("fsdp", "cp", None),
            P("fsdp", "cp", None),
        ),
        out_specs=(
            P("fsdp", "cp", None),
            P("fsdp", "cp", None),
            P("fsdp", "cp", None),
            P("fsdp", "cp"),
        ),
        check_vma=False,
    )
```

profile of v0, /device:TPU:0, one launch (start us, length us, event | category | flops | bytes accessed | tf_op | source)
XLA Modules:
  0.0 243.9 jit_solution(6406590973211021745)
XLA Ops:
  7.3 0.7 copy.51
  8.0 14.8 %all_gather.6 = f32[1,512,10]{1,2,0:T(8,128)S(1)} all-gather(f32[1,128,10]{1,2,0:T(8,128)S(1)} %copy.51), channel_id=1, replica_groups=mesh['fsdp'=8,'cp'=4] {'cp'}, dimensions={1}, use_global_device_ids=true | all-gather | bytes 25600 | tf_op jit(solution)/shard_map/all_gather | solution.py:28
  22.8 1.2 copy.56
  24.0 1.9 copy.55
  25.9 1.2 copy.50
  27.1 0.2 copy.57
  27.3 1.2 copy.52
  28.5 0.9 copy.58
  29.4 1.2 copy.54
  30.7 13.1 %all-gather = f32[512,10]{0,1:T(8,128)S(1)} all-gather(f32[128,10]{0,1:T(8,128)S(1)} %reduce_sum.11), channel_id=2, replica_groups=mesh['fsdp'=8,'cp'=4] {'cp'}, dimensions={0}, use_global_device_ids=true | all-gather | bytes 25600 | tf_op jit(solution)/shard_map/all_gather | solution.py:29
  43.8 87.0 %while.24 = (s32[]{:T(128)}, bf16[1,128,1280]{1,2,0:T(8,128)(2,1)}, bf16[1,128,1280]{1,2,0:T(8,128)(2,1)S(1)}, f32[128,10,128]{2,0,1:T(8,128)}, f32[128,10,128]{...) while((s32[]{:T(128)}, bf16[1,128,1280]{1,2,0:T(8,128)(2,1)}, ...), condition=%wide.region_2.3_spmd.clone, body=%wide.region_1.2_spmd.clone.sunk | while | flops 212008976 | bytes 15104460 | solution.py:71
  43.8 1.0 copy.81
  44.8 1.6 collective-permute-start
  46.5 0.4 fusion.46
  46.9 1.4 fusion.47
  48.3 1.0 fusion.48
  49.2 2.9 %collective-permute-start.2 = (bf16[128,10,128]{2,0,1:T(8,128)(2,1)}, bf16[128,10,128]{2,0,1:T(8,128)(2,1)}, u32[]{:S(2)}, u32[]{:S(2)}) collective-permute-start(bf16[128,10,128]{2,0,1:T(8,128)(2,1)} %fusion.48), channel_id=1, source_target_pairs={{0,1},{1,2},{2,3},{3,0},{4,5},{5,6},{6,7},{7,4},{8,9},{9,10},{10,1... | collective-permute-start | bytes 983048 | tf_op jit(solution)/shard_map/while/body/eval_jaxpr/ppermute | solution.py:10
  52.1 1.2 fusion.49
  53.4 0.4 fusion.50
  53.8 11.1 %collective-permute-done.2 = bf16[128,10,128]{2,0,1:T(8,128)(2,1)} collective-permute-done((bf16[128,10,128]{2,0,1:T(8,128)(2,1)}, bf16[128,10,128]{2,0,1:T(8,128)(2,1)}, u32[]{:S(2)}, u32[]{:S(2)}) %collective-permute-start.2) | collective-permute-done | bytes 327712 | tf_op jit(solution)/shard_map/while/body/eval_jaxpr/ppermute | solution.py:10
  64.8 1.9 convert_element_type.94
  66.8 1.0 copy.81
  67.8 1.1 collective-permute-start.1
  69.0 0.4 fusion.46
  69.3 1.4 fusion.47
  70.7 2.1 fusion.48
  72.8 2.5 %collective-permute-start.2 = (bf16[128,10,128]{2,0,1:T(8,128)(2,1)}, bf16[128,10,128]{2,0,1:T(8,128)(2,1)}, u32[]{:S(2)}, u32[]{:S(2)}) collective-permute-start(bf16[128,10,128]{2,0,1:T(8,128)(2,1)} %fusion.48), channel_id=1, source_target_pairs={{0,1},{1,2},{2,3},{3,0},{4,5},{5,6},{6,7},{7,4},{8,9},{9,10},{10,1... | collective-permute-start | bytes 983048 | tf_op jit(solution)/shard_map/while/body/eval_jaxpr/ppermute | solution.py:10
  75.2 2.3 fusion.49
  77.6 0.4 fusion.50
  78.0 8.8 %collective-permute-done.2 = bf16[128,10,128]{2,0,1:T(8,128)(2,1)} collective-permute-done((bf16[128,10,128]{2,0,1:T(8,128)(2,1)}, bf16[128,10,128]{2,0,1:T(8,128)(2,1)}, u32[]{:S(2)}, u32[]{:S(2)}) %collective-permute-start.2) | collective-permute-done | bytes 327712 | tf_op jit(solution)/shard_map/while/body/eval_jaxpr/ppermute | solution.py:10
  86.8 1.9 convert_element_type.94
  88.7 1.0 copy.81
  89.7 1.2 collective-permute-start.1
  90.9 0.4 fusion.46
  91.3 1.4 fusion.47
  92.6 2.1 fusion.48
  94.7 2.5 %collective-permute-start.2 = (bf16[128,10,128]{2,0,1:T(8,128)(2,1)}, bf16[128,10,128]{2,0,1:T(8,128)(2,1)}, u32[]{:S(2)}, u32[]{:S(2)}) collective-permute-start(bf16[128,10,128]{2,0,1:T(8,128)(2,1)} %fusion.48), channel_id=1, source_target_pairs={{0,1},{1,2},{2,3},{3,0},{4,5},{5,6},{6,7},{7,4},{8,9},{9,10},{10,1... | collective-permute-start | bytes 983048 | tf_op jit(solution)/shard_map/while/body/eval_jaxpr/ppermute | solution.py:10
  97.2 2.3 fusion.49
  99.5 0.4 fusion.50
  99.9 8.8 %collective-permute-done.2 = bf16[128,10,128]{2,0,1:T(8,128)(2,1)} collective-permute-done((bf16[128,10,128]{2,0,1:T(8,128)(2,1)}, bf16[128,10,128]{2,0,1:T(8,128)(2,1)}, u32[]{:S(2)}, u32[]{:S(2)}) %collective-permute-start.2) | collective-permute-done | bytes 327712 | tf_op jit(solution)/shard_map/while/body/eval_jaxpr/ppermute | solution.py:10
  108.7 1.9 convert_element_type.94
  110.6 1.0 copy.81
  111.6 1.2 collective-permute-start.1
  112.8 0.4 fusion.46
  113.2 1.4 fusion.47
  114.5 2.1 fusion.48
  116.6 2.5 %collective-permute-start.2 = (bf16[128,10,128]{2,0,1:T(8,128)(2,1)}, bf16[128,10,128]{2,0,1:T(8,128)(2,1)}, u32[]{:S(2)}, u32[]{:S(2)}) collective-permute-start(bf16[128,10,128]{2,0,1:T(8,128)(2,1)} %fusion.48), channel_id=1, source_target_pairs={{0,1},{1,2},{2,3},{3,0},{4,5},{5,6},{6,7},{7,4},{8,9},{9,10},{10,1... | collective-permute-start | bytes 983048 | tf_op jit(solution)/shard_map/while/body/eval_jaxpr/ppermute | solution.py:10
  119.1 2.3 fusion.49
  121.4 0.4 fusion.50
  121.8 7.1 %collective-permute-done.2 = bf16[128,10,128]{2,0,1:T(8,128)(2,1)} collective-permute-done((bf16[128,10,128]{2,0,1:T(8,128)(2,1)}, bf16[128,10,128]{2,0,1:T(8,128)(2,1)}, u32[]{:S(2)}, u32[]{:S(2)}) %collective-permute-start.2) | collective-permute-done | bytes 327712 | tf_op jit(solution)/shard_map/while/body/eval_jaxpr/ppermute | solution.py:10
  128.9 1.9 convert_element_type.94
  130.8 0.2 copy.61
  131.0 4.6 %fusion.9 = bf16[2560,1280]{0,1:T(8,128)(2,1)} fusion(bf16[128,1280]{0,1:T(8,128)(2,1)S(1)} %bitcast.82, bf16[1,128,2560]{2,1,0:T(8,128)(2,1)S(1)} %copy-done), kind=kOutput, calls=%fused_computation.17 | convolution fusion | flops 842137600 | bytes 7536640 | tf_op jit(solution)/shard_map/tf,tw->fw/dot_general | solution.py:78
  135.6 9.5 %copy.72 = bf16[2560,1280]{1,0:T(8,128)(2,1)} copy(bf16[2560,1280]{0,1:T(8,128)(2,1)} %fusion.9) | data formatting | bytes 13107200
  145.2 61.4 %reduce-scatter.7.cloned.1.call-done = bf16[320,1280]{1,0:T(8,128)(2,1)} async-done(((bf16[2560,1280]{1,0:T(8,128)(2,1)}), bf16[320,1280]{1,0:T(8,128)(2,1)}) %reduce-scatter.7.cloned.1.call-update) | async-done | bytes 819216
  206.5 2.2 copy.73
  208.8 0.2 copy.59
  209.0 0.1 multiply_convert_fusion.1
  209.1 0.9 copy.62
  210.0 0.9 copy.64
  210.9 0.2 copy.60
  211.2 0.9 copy.63
  212.1 23.1 %reduce-scatter.5.cloned.1.call-done = bf16[320,320]{0,1:T(8,128)(2,1)} async-done(((bf16[320,1280]{0,1:T(8,128)(2,1)}), bf16[320,320]{0,1:T(8,128)(2,1)}) %reduce-scatter.5.cloned.1.call-update) | async-done | bytes 204816 | tf_op jit(solution)/shard_map/reduce_scatter | solution.py:85
  235.2 1.9 copy.65
  (36 shorter events, 0.6 us)
Async XLA Ops:
  7.2 123.9 %copy-start = (bf16[1,128,2560]{2,1,0:T(8,128)(2,1)S(1)}, bf16[1,128,2560]{2,1,0:T(8,128)(2,1)}, u32[]{:S(2)}) copy-start(bf16[1,128,2560]{2,1,0:T(8,128)(2,1)} %param.9) | copy-start | bytes 1966084
  7.2 199.4 %reduce-scatter.7.cloned.1.call-start = ((), (), s32[]{:S(2)}) async-start(), calls=%async_computation.3 | async-start | bytes 7372800
  44.8 21.9 %collective-permute-start = (bf16[1,128,1280]{1,2,0:T(8,128)(2,1)S(1)}, bf16[1,128,1280]{1,2,0:T(8,128)(2,1)}, u32[]{:S(2)}, u32[]{:S(2)}) collective-permute-start(bf16[1,128,1280]{1,2,0:T(8,128)(2,1)S(1)} %copy.81), channel_id=1, source_target_pairs={{0,1},{1,2},{2,3},{3,0},{4,5},{5,6},{6,7},{7,4},{8,9},{9,10},{10,1... | collective-permute-start | bytes 983048 | tf_op jit(solution)/shard_map/while/body/eval_jaxpr/ppermute | solution.py:10
  46.4 20.4 %collective-permute-start.1 = (bf16[1,128,1280]{1,2,0:T(8,128)(2,1)S(1)}, bf16[1,128,1280]{1,2,0:T(8,128)(2,1)S(1)}, u32[]{:S(2)}, u32[]{:S(2)}) collective-permute-start(bf16[1,128,1280]{1,2,0:T(8,128)(2,1)S(1)} %copy.82), channel_id=1, source_target_pairs={{0,1},{1,2},{2,3},{3,0},{4,5},{5,6},{6,7},{7,4},{8,9},{9,10},{10,1... | collective-permute-start | bytes 983048 | tf_op jit(solution)/shard_map/while/body/eval_jaxpr/ppermute | solution.py:10
  49.2 15.6 %collective-permute-start.2 = (bf16[128,10,128]{2,0,1:T(8,128)(2,1)}, bf16[128,10,128]{2,0,1:T(8,128)(2,1)}, u32[]{:S(2)}, u32[]{:S(2)}) collective-permute-start(bf16[128,10,128]{2,0,1:T(8,128)(2,1)} %fusion.48), channel_id=1, source_target_pairs={{0,1},{1,2},{2,3},{3,0},{4,5},{5,6},{6,7},{7,4},{8,9},{9,10},{10,1... | collective-permute-start | bytes 983048 | tf_op jit(solution)/shard_map/while/body/eval_jaxpr/ppermute | solution.py:10
  67.7 20.9 %collective-permute-start = (bf16[1,128,1280]{1,2,0:T(8,128)(2,1)S(1)}, bf16[1,128,1280]{1,2,0:T(8,128)(2,1)}, u32[]{:S(2)}, u32[]{:S(2)}) collective-permute-start(bf16[1,128,1280]{1,2,0:T(8,128)(2,1)S(1)} %copy.81), channel_id=1, source_target_pairs={{0,1},{1,2},{2,3},{3,0},{4,5},{5,6},{6,7},{7,4},{8,9},{9,10},{10,1... | collective-permute-start | bytes 983048 | tf_op jit(solution)/shard_map/while/body/eval_jaxpr/ppermute | solution.py:10
  67.8 20.9 %collective-permute-start.1 = (bf16[1,128,1280]{1,2,0:T(8,128)(2,1)S(1)}, bf16[1,128,1280]{1,2,0:T(8,128)(2,1)S(1)}, u32[]{:S(2)}, u32[]{:S(2)}) collective-permute-start(bf16[1,128,1280]{1,2,0:T(8,128)(2,1)S(1)} %copy.82), channel_id=1, source_target_pairs={{0,1},{1,2},{2,3},{3,0},{4,5},{5,6},{6,7},{7,4},{8,9},{9,10},{10,1... | collective-permute-start | bytes 983048 | tf_op jit(solution)/shard_map/while/body/eval_jaxpr/ppermute | solution.py:10
  72.8 14.0 %collective-permute-start.2 = (bf16[128,10,128]{2,0,1:T(8,128)(2,1)}, bf16[128,10,128]{2,0,1:T(8,128)(2,1)}, u32[]{:S(2)}, u32[]{:S(2)}) collective-permute-start(bf16[128,10,128]{2,0,1:T(8,128)(2,1)} %fusion.48), channel_id=1, source_target_pairs={{0,1},{1,2},{2,3},{3,0},{4,5},{5,6},{6,7},{7,4},{8,9},{9,10},{10,1... | collective-permute-start | bytes 983048 | tf_op jit(solution)/shard_map/while/body/eval_jaxpr/ppermute | solution.py:10
  89.7 20.9 %collective-permute-start = (bf16[1,128,1280]{1,2,0:T(8,128)(2,1)S(1)}, bf16[1,128,1280]{1,2,0:T(8,128)(2,1)}, u32[]{:S(2)}, u32[]{:S(2)}) collective-permute-start(bf16[1,128,1280]{1,2,0:T(8,128)(2,1)S(1)} %copy.81), channel_id=1, source_target_pairs={{0,1},{1,2},{2,3},{3,0},{4,5},{5,6},{6,7},{7,4},{8,9},{9,10},{10,1... | collective-permute-start | bytes 983048 | tf_op jit(solution)/shard_map/while/body/eval_jaxpr/ppermute | solution.py:10
  89.7 20.9 %collective-permute-start.1 = (bf16[1,128,1280]{1,2,0:T(8,128)(2,1)S(1)}, bf16[1,128,1280]{1,2,0:T(8,128)(2,1)S(1)}, u32[]{:S(2)}, u32[]{:S(2)}) collective-permute-start(bf16[1,128,1280]{1,2,0:T(8,128)(2,1)S(1)} %copy.82), channel_id=1, source_target_pairs={{0,1},{1,2},{2,3},{3,0},{4,5},{5,6},{6,7},{7,4},{8,9},{9,10},{10,1... | collective-permute-start | bytes 983048 | tf_op jit(solution)/shard_map/while/body/eval_jaxpr/ppermute | solution.py:10
  94.7 14.0 %collective-permute-start.2 = (bf16[128,10,128]{2,0,1:T(8,128)(2,1)}, bf16[128,10,128]{2,0,1:T(8,128)(2,1)}, u32[]{:S(2)}, u32[]{:S(2)}) collective-permute-start(bf16[128,10,128]{2,0,1:T(8,128)(2,1)} %fusion.48), channel_id=1, source_target_pairs={{0,1},{1,2},{2,3},{3,0},{4,5},{5,6},{6,7},{7,4},{8,9},{9,10},{10,1... | collective-permute-start | bytes 983048 | tf_op jit(solution)/shard_map/while/body/eval_jaxpr/ppermute | solution.py:10
  111.6 19.2 %collective-permute-start = (bf16[1,128,1280]{1,2,0:T(8,128)(2,1)S(1)}, bf16[1,128,1280]{1,2,0:T(8,128)(2,1)}, u32[]{:S(2)}, u32[]{:S(2)}) collective-permute-start(bf16[1,128,1280]{1,2,0:T(8,128)(2,1)S(1)} %copy.81), channel_id=1, source_target_pairs={{0,1},{1,2},{2,3},{3,0},{4,5},{5,6},{6,7},{7,4},{8,9},{9,10},{10,1... | collective-permute-start | bytes 983048 | tf_op jit(solution)/shard_map/while/body/eval_jaxpr/ppermute | solution.py:10
  111.6 19.2 %collective-permute-start.1 = (bf16[1,128,1280]{1,2,0:T(8,128)(2,1)S(1)}, bf16[1,128,1280]{1,2,0:T(8,128)(2,1)S(1)}, u32[]{:S(2)}, u32[]{:S(2)}) collective-permute-start(bf16[1,128,1280]{1,2,0:T(8,128)(2,1)S(1)} %copy.82), channel_id=1, source_target_pairs={{0,1},{1,2},{2,3},{3,0},{4,5},{5,6},{6,7},{7,4},{8,9},{9,10},{10,1... | collective-permute-start | bytes 983048 | tf_op jit(solution)/shard_map/while/body/eval_jaxpr/ppermute | solution.py:10
  116.6 12.3 %collective-permute-start.2 = (bf16[128,10,128]{2,0,1:T(8,128)(2,1)}, bf16[128,10,128]{2,0,1:T(8,128)(2,1)}, u32[]{:S(2)}, u32[]{:S(2)}) collective-permute-start(bf16[128,10,128]{2,0,1:T(8,128)(2,1)} %fusion.48), channel_id=1, source_target_pairs={{0,1},{1,2},{2,3},{3,0},{4,5},{5,6},{6,7},{7,4},{8,9},{9,10},{10,1... | collective-permute-start | bytes 983048 | tf_op jit(solution)/shard_map/while/body/eval_jaxpr/ppermute | solution.py:10
  145.1 63.7 %copy-start.2 = (f32[128,10,128]{2,0,1:T(8,128)S(1)}, f32[128,10,128]{2,0,1:T(8,128)}, u32[]{:S(2)}) copy-start(f32[128,10,128]{2,0,1:T(8,128)} %get-tuple-element.271) | copy-start | bytes 1966084
  145.1 65.8 %copy-start.1 = (f32[128,10,128]{2,0,1:T(8,128)S(1)}, f32[128,10,128]{2,0,1:T(8,128)}, u32[]{:S(2)}) copy-start(f32[128,10,128]{2,0,1:T(8,128)} %get-tuple-element.272) | copy-start | bytes 1966084
  145.1 90.1 %reduce-scatter.5.cloned.1.call-start = ((), (), s32[]{:S(2)}) async-start(), calls=%async_computation.2 | async-start | bytes 1228800 | tf_op jit(solution)/shard_map/reduce_scatter | solution.py:85
Sparse Core Ops, SparseCore 0:
  145.2 61.2 reduce-scatter.6
  208.9 26.2 reduce-scatter.4
where the time goes:
time: 245 us; the launch traced here: 244 us
  waiting for transfers between devices  120 us (49%)
  local copies, waits for them, and re-layouts  29.4 us (12%)
  matrix products  28.4 us (12%)
  blocking collectives  28 us (11%)
  starting transfers between devices  15.6 us (6%)
  between operations  14.2 us (6%)
  other arithmetic  7.92 us (3%)
    unnamed x3, waiting for transfers between devices  61.4 us
    ppermute x12, waiting for transfers between devices, passed_along(): return lax.ppermute(value, axis, pairs)  35.8 us
    unnamed x20, local copies, waits for them, and re-layouts  24.8 us
    reduce_scatter x1, waiting for transfers between devices, on_device(): lax.psum_scatter(row_sums, 'cp', scatter_dimension=1, tiled=True)  23.1 us
    ppermute x12, starting transfers between devices, passed_along(): return lax.ppermute(value, axis, pairs)  15.5 us
    all_gather x1, blocking collectives, on_device(): lax.all_gather(log_sums, 'cp', axis=1, tiled=True)  14.8 us
    all_gather x1, blocking collectives, on_device(): lax.all_gather(row_delta, 'cp', axis=1, tiled=True)  13.1 us
    dot_general x4, matrix products, cycle_step(): jnp.einsum('hqk,qhd->khd', grad_score, query_heads, preferred_element_typ...  8.16 us
  transfers between devices with their start and end apart: 14, of which 6 were waited for; matrix products, arithmetic and copies ran while one was open for 14% of the time, Pallas kernels for 0%

commit v1 on v0

--- a/solution.py
+++ b/solution.py
@@ -25,7 +25,9 @@
     own_key = as_heads(key_rows)
     own_value = as_heads(value_rows)
     all_norms, all_deltas = (
-        lax.all_gather(log_sums, "cp", axis=1, tiled=True),
+        jnp.concatenate(
+            lax.all_to_all(jnp.stack([log_sums] * lax.axis_size("cp")), "cp", 0, 0), axis=1
+        ),
         lax.all_gather(row_delta, "cp", axis=1, tiled=True),
     )
 

time: 245 us -> 244 us (level)
  blocking collectives: 28 us -> 13.7 us
  waiting for transfers between devices: 120 us -> 134 us
    all_gather x1 -> x0, blocking collectives: 14.8 us -> none  [on_device(): lax.all_gather(log_sums, 'cp', axis=1, tiled=True)]
    ppermute x12, waiting for transfers between devices: 35.8 us -> 49.2 us  [passed_along(): return lax.ppermute(value, axis, pairs)]
    ppermute x12, starting transfers between devices: 15.5 us -> 8.53 us  [passed_along(): return lax.ppermute(value, axis, pairs)]
    all_to_all x0 -> x1, starting transfers between devices: none -> 6.35 us  [on_device(): lax.all_to_all(jnp.stack([log_sums] * lax.axis_size('cp')), 'cp', 0, 0)]
  transfers between devices with their start and end apart: 14 -> 15, of which waited for: 6 -> 6; matrix products, arithmetic and copies ran while one was open for 14% -> 18% of each run, Pallas kernels for 0% -> 0%
where the time goes in v1:
time: 244 us; the launch traced here: 243 us
  waiting for transfers between devices  134 us (55%)
  local copies, waits for them, and re-layouts  30.2 us (12%)
  matrix products  28.4 us (12%)
  starting transfers between devices  14.9 us (6%)
  between operations  14.2 us (6%)
  blocking collectives  13.7 us (6%)
  other arithmetic  7.89 us (3%)
    unnamed x3, waiting for transfers between devices  61.4 us
    ppermute x12, waiting for transfers between devices, passed_along(): return lax.ppermute(value, axis, pairs)  49.2 us
    unnamed x20, local copies, waits for them, and re-layouts  24.8 us
    reduce_scatter x1, waiting for transfers between devices, on_device(): lax.psum_scatter(row_sums, 'cp', scatter_dimension=1, tiled=True)  23 us
    all_gather x1, blocking collectives, on_device(): lax.all_gather(row_delta, 'cp', axis=1, tiled=True)  13.7 us
    ppermute x12, starting transfers between devices, passed_along(): return lax.ppermute(value, axis, pairs)  8.53 us
    dot_general x4, matrix products, cycle_step(): jnp.einsum('hqk,qhd->khd', grad_score, query_heads, preferred_element_typ...  8.13 us
    convert_element_type x4, other arithmetic, cycle_step(): passed_along(query_run.astype(jnp.bfloat16), 'cp', 1)  7.62 us
  transfers between devices with their start and end apart: 15, of which 6 were waited for; matrix products, arithmetic and copies ran while one was open for 18% of the time, Pallas kernels for 0%

profile of v1, /device:TPU:0, one launch (start us, length us, event | category | flops | bytes accessed | tf_op | source)
XLA Modules:
  0.0 243.1 jit_solution(9632144444445845076)
XLA Ops:
  7.2 0.8 copy.79
  7.9 0.6 stack.2
  8.6 6.3 %all-to-all-start = ((f32[4,1,128,10]{2,1,3,0:T(1,128)}), f32[4,1,128,10]{2,1,3,0:T(1,128)S(1)}, u32[]{:S(2)}, u32[]{:S(2)}) async-start(f32[4,1,128,10]{2,1,3,0:T(1,128)} %stack.2), calls=%async_computation | async-start | bytes 40960 | tf_op jit(solution)/shard_map/all_to_all | solution.py:29
  14.9 1.2 copy.55
  16.1 1.2 copy.53
  17.4 1.9 copy.54
  19.3 1.2 copy.49
  20.4 0.2 copy.56
  20.7 1.2 copy.51
  21.9 0.9 copy.58
  22.8 13.7 %all-gather = f32[512,10]{0,1:T(8,128)S(1)} all-gather(f32[128,10]{0,1:T(8,128)S(1)} %reduce_sum.11), channel_id=2, replica_groups=mesh['fsdp'=8,'cp'=4] {'cp'}, dimensions={0}, use_global_device_ids=true | all-gather | bytes 25600 | tf_op jit(solution)/shard_map/all_gather | solution.py:31
  36.5 93.6 %while.24 = (s32[]{:T(128)}, bf16[1,128,1280]{1,2,0:T(8,128)(2,1)}, bf16[1,128,1280]{1,2,0:T(8,128)(2,1)S(1)}, f32[128,10,128]{2,0,1:T(8,128)}, f32[128,10,128]{...) while((s32[]{:T(128)}, bf16[1,128,1280]{1,2,0:T(8,128)(2,1)}, ...), condition=%wide.region_2.3_spmd.clone, body=%wide.region_1.2_spmd.clone.sunk | while | flops 212008976 | bytes 15114704 | solution.py:73
  36.5 1.0 copy.89
  37.5 1.5 collective-permute-start
  39.2 0.4 fusion.46
  39.5 1.4 fusion.47
  40.9 1.0 fusion.48
  41.9 2.9 %collective-permute-start.2 = (bf16[128,10,128]{2,0,1:T(8,128)(2,1)}, bf16[128,10,128]{2,0,1:T(8,128)(2,1)}, u32[]{:S(2)}, u32[]{:S(2)}) collective-permute-start(bf16[128,10,128]{2,0,1:T(8,128)(2,1)} %fusion.48), channel_id=1, source_target_pairs={{0,1},{1,2},{2,3},{3,0},{4,5},{5,6},{6,7},{7,4},{8,9},{9,10},{10,1... | collective-permute-start | bytes 983048 | tf_op jit(solution)/shard_map/while/body/eval_jaxpr/ppermute | solution.py:10
  44.7 1.2 fusion.49
  46.0 0.4 fusion.50
  46.4 13.1 %collective-permute-done.2 = bf16[128,10,128]{2,0,1:T(8,128)(2,1)} collective-permute-done((bf16[128,10,128]{2,0,1:T(8,128)(2,1)}, bf16[128,10,128]{2,0,1:T(8,128)(2,1)}, u32[]{:S(2)}, u32[]{:S(2)}) %collective-permute-start.2) | collective-permute-done | bytes 327712 | tf_op jit(solution)/shard_map/while/body/eval_jaxpr/ppermute | solution.py:10
  59.5 1.9 convert_element_type.94
  61.4 1.0 copy.89
  62.4 0.2 collective-permute-start.1
  62.6 0.4 fusion.46
  63.0 1.4 fusion.47
  64.3 2.1 fusion.48
  66.4 2.5 %collective-permute-start.2 = (bf16[128,10,128]{2,0,1:T(8,128)(2,1)}, bf16[128,10,128]{2,0,1:T(8,128)(2,1)}, u32[]{:S(2)}, u32[]{:S(2)}) collective-permute-start(bf16[128,10,128]{2,0,1:T(8,128)(2,1)} %fusion.48), channel_id=1, source_target_pairs={{0,1},{1,2},{2,3},{3,0},{4,5},{5,6},{6,7},{7,4},{8,9},{9,10},{10,1... | collective-permute-start | bytes 983048 | tf_op jit(solution)/shard_map/while/body/eval_jaxpr/ppermute | solution.py:10
  68.9 2.3 fusion.49
  71.2 0.4 fusion.50
  71.6 11.8 %collective-permute-done.2 = bf16[128,10,128]{2,0,1:T(8,128)(2,1)} collective-permute-done((bf16[128,10,128]{2,0,1:T(8,128)(2,1)}, bf16[128,10,128]{2,0,1:T(8,128)(2,1)}, u32[]{:S(2)}, u32[]{:S(2)}) %collective-permute-start.2) | collective-permute-done | bytes 327712 | tf_op jit(solution)/shard_map/while/body/eval_jaxpr/ppermute | solution.py:10
  83.3 1.9 convert_element_type.94
  85.2 1.0 copy.89
  86.4 0.4 fusion.46
  86.8 1.4 fusion.47
  88.1 2.1 fusion.48
  90.2 0.7 collective-permute-start.2
  90.9 2.3 fusion.49
  93.2 0.4 fusion.50
  93.6 12.6 %collective-permute-done.2 = bf16[128,10,128]{2,0,1:T(8,128)(2,1)} collective-permute-done((bf16[128,10,128]{2,0,1:T(8,128)(2,1)}, bf16[128,10,128]{2,0,1:T(8,128)(2,1)}, u32[]{:S(2)}, u32[]{:S(2)}) %collective-permute-start.2) | collective-permute-done | bytes 327712 | tf_op jit(solution)/shard_map/while/body/eval_jaxpr/ppermute | solution.py:10
  106.2 1.9 convert_element_type.94
  108.2 1.0 copy.89
  109.3 0.4 fusion.46
  109.7 1.4 fusion.47
  111.0 2.1 fusion.48
  113.1 0.6 collective-permute-start.2
  113.7 2.3 fusion.49
  116.0 0.4 fusion.50
  116.4 11.8 %collective-permute-done.2 = bf16[128,10,128]{2,0,1:T(8,128)(2,1)} collective-permute-done((bf16[128,10,128]{2,0,1:T(8,128)(2,1)}, bf16[128,10,128]{2,0,1:T(8,128)(2,1)}, u32[]{:S(2)}, u32[]{:S(2)}) %collective-permute-start.2) | collective-permute-done | bytes 327712 | tf_op jit(solution)/shard_map/while/body/eval_jaxpr/ppermute | solution.py:10
  128.2 1.9 convert_element_type.94
  130.1 0.2 copy.61
  130.3 4.6 %fusion.9 = bf16[2560,1280]{0,1:T(8,128)(2,1)} fusion(bf16[128,1280]{0,1:T(8,128)(2,1)S(1)} %bitcast.89, bf16[1,128,2560]{2,1,0:T(8,128)(2,1)S(1)} %copy-done), kind=kOutput, calls=%fused_computation.18 | convolution fusion | flops 842137600 | bytes 7536640 | tf_op jit(solution)/shard_map/tf,tw->fw/dot_general | solution.py:80
  134.9 9.5 %copy.72 = bf16[2560,1280]{1,0:T(8,128)(2,1)} copy(bf16[2560,1280]{0,1:T(8,128)(2,1)} %fusion.9) | data formatting | bytes 13107200
  144.5 61.3 %reduce-scatter.7.cloned.1.call-done = bf16[320,1280]{1,0:T(8,128)(2,1)} async-done(((bf16[2560,1280]{1,0:T(8,128)(2,1)}), bf16[320,1280]{1,0:T(8,128)(2,1)}) %reduce-scatter.7.cloned.1.call-update) | async-done | bytes 819216
  205.8 2.2 copy.73
  208.0 0.2 copy.59
  208.3 0.1 multiply_convert_fusion.1
  208.4 0.9 copy.62
  209.3 0.9 copy.64
  210.2 0.2 copy.60
  210.4 0.1 multiply_convert_fusion
  210.5 0.9 copy.63
  211.4 23.0 %reduce-scatter.5.cloned.1.call-done = bf16[320,320]{0,1:T(8,128)(2,1)} async-done(((bf16[320,1280]{0,1:T(8,128)(2,1)}), bf16[320,320]{0,1:T(8,128)(2,1)}) %reduce-scatter.5.cloned.1.call-update) | async-done | bytes 204816 | tf_op jit(solution)/shard_map/reduce_scatter | solution.py:87
  234.4 1.9 copy.65
  (47 shorter events, 0.6 us)
Async XLA Ops:
  7.2 123.2 %copy-start = (bf16[1,128,2560]{2,1,0:T(8,128)(2,1)S(1)}, bf16[1,128,2560]{2,1,0:T(8,128)(2,1)}, u32[]{:S(2)}) copy-start(bf16[1,128,2560]{2,1,0:T(8,128)(2,1)} %param.9) | copy-start | bytes 1966084
  8.6 27.9 %all-to-all-start = ((f32[4,1,128,10]{2,1,3,0:T(1,128)}), f32[4,1,128,10]{2,1,3,0:T(1,128)S(1)}, u32[]{:S(2)}, u32[]{:S(2)}) async-start(f32[4,1,128,10]{2,1,3,0:T(1,128)} %stack.2), calls=%async_computation | async-start | bytes 40960 | tf_op jit(solution)/shard_map/all_to_all | solution.py:29
  14.9 190.9 %reduce-scatter.7.cloned.1.call-start = ((), (), s32[]{:S(2)}) async-start(), calls=%async_computation.4 | async-start | bytes 7372800
  37.5 23.9 %collective-permute-start = (bf16[1,128,1280]{1,2,0:T(8,128)(2,1)S(1)}, bf16[1,128,1280]{1,2,0:T(8,128)(2,1)}, u32[]{:S(2)}, u32[]{:S(2)}) collective-permute-start(bf16[1,128,1280]{1,2,0:T(8,128)(2,1)S(1)} %copy.89), channel_id=1, source_target_pairs={{0,1},{1,2},{2,3},{3,0},{4,5},{5,6},{6,7},{7,4},{8,9},{9,10},{10,1... | collective-permute-start | bytes 983048 | tf_op jit(solution)/shard_map/while/body/eval_jaxpr/ppermute | solution.py:10
  39.0 22.4 %collective-permute-start.1 = (bf16[1,128,1280]{1,2,0:T(8,128)(2,1)S(1)}, bf16[1,128,1280]{1,2,0:T(8,128)(2,1)S(1)}, u32[]{:S(2)}, u32[]{:S(2)}) collective-permute-start(bf16[1,128,1280]{1,2,0:T(8,128)(2,1)S(1)} %copy.90), channel_id=1, source_target_pairs={{0,1},{1,2},{2,3},{3,0},{4,5},{5,6},{6,7},{7,4},{8,9},{9,10},{10,1... | collective-permute-start | bytes 983048 | tf_op jit(solution)/shard_map/while/body/eval_jaxpr/ppermute | solution.py:10
  41.9 17.6 %collective-permute-start.2 = (bf16[128,10,128]{2,0,1:T(8,128)(2,1)}, bf16[128,10,128]{2,0,1:T(8,128)(2,1)}, u32[]{:S(2)}, u32[]{:S(2)}) collective-permute-start(bf16[128,10,128]{2,0,1:T(8,128)(2,1)} %fusion.48), channel_id=1, source_target_pairs={{0,1},{1,2},{2,3},{3,0},{4,5},{5,6},{6,7},{7,4},{8,9},{9,10},{10,1... | collective-permute-start | bytes 983048 | tf_op jit(solution)/shard_map/while/body/eval_jaxpr/ppermute | solution.py:10
  62.3 22.9 %collective-permute-start = (bf16[1,128,1280]{1,2,0:T(8,128)(2,1)S(1)}, bf16[1,128,1280]{1,2,0:T(8,128)(2,1)}, u32[]{:S(2)}, u32[]{:S(2)}) collective-permute-start(bf16[1,128,1280]{1,2,0:T(8,128)(2,1)S(1)} %copy.89), channel_id=1, source_target_pairs={{0,1},{1,2},{2,3},{3,0},{4,5},{5,6},{6,7},{7,4},{8,9},{9,10},{10,1... | collective-permute-start | bytes 983048 | tf_op jit(solution)/shard_map/while/body/eval_jaxpr/ppermute | solution.py:10
  62.4 22.9 %collective-permute-start.1 = (bf16[1,128,1280]{1,2,0:T(8,128)(2,1)S(1)}, bf16[1,128,1280]{1,2,0:T(8,128)(2,1)S(1)}, u32[]{:S(2)}, u32[]{:S(2)}) collective-permute-start(bf16[1,128,1280]{1,2,0:T(8,128)(2,1)S(1)} %copy.90), channel_id=1, source_target_pairs={{0,1},{1,2},{2,3},{3,0},{4,5},{5,6},{6,7},{7,4},{8,9},{9,10},{10,1... | collective-permute-start | bytes 983048 | tf_op jit(solution)/shard_map/while/body/eval_jaxpr/ppermute | solution.py:10
  66.4 17.0 %collective-permute-start.2 = (bf16[128,10,128]{2,0,1:T(8,128)(2,1)}, bf16[128,10,128]{2,0,1:T(8,128)(2,1)}, u32[]{:S(2)}, u32[]{:S(2)}) collective-permute-start(bf16[128,10,128]{2,0,1:T(8,128)(2,1)} %fusion.48), channel_id=1, source_target_pairs={{0,1},{1,2},{2,3},{3,0},{4,5},{5,6},{6,7},{7,4},{8,9},{9,10},{10,1... | collective-permute-start | bytes 983048 | tf_op jit(solution)/shard_map/while/body/eval_jaxpr/ppermute | solution.py:10
  86.2 21.9 %collective-permute-start = (bf16[1,128,1280]{1,2,0:T(8,128)(2,1)S(1)}, bf16[1,128,1280]{1,2,0:T(8,128)(2,1)}, u32[]{:S(2)}, u32[]{:S(2)}) collective-permute-start(bf16[1,128,1280]{1,2,0:T(8,128)(2,1)S(1)} %copy.89), channel_id=1, source_target_pairs={{0,1},{1,2},{2,3},{3,0},{4,5},{5,6},{6,7},{7,4},{8,9},{9,10},{10,1... | collective-permute-start | bytes 983048 | tf_op jit(solution)/shard_map/while/body/eval_jaxpr/ppermute | solution.py:10
  86.2 21.9 %collective-permute-start.1 = (bf16[1,128,1280]{1,2,0:T(8,128)(2,1)S(1)}, bf16[1,128,1280]{1,2,0:T(8,128)(2,1)S(1)}, u32[]{:S(2)}, u32[]{:S(2)}) collective-permute-start(bf16[1,128,1280]{1,2,0:T(8,128)(2,1)S(1)} %copy.90), channel_id=1, source_target_pairs={{0,1},{1,2},{2,3},{3,0},{4,5},{5,6},{6,7},{7,4},{8,9},{9,10},{10,1... | collective-permute-start | bytes 983048 | tf_op jit(solution)/shard_map/while/body/eval_jaxpr/ppermute | solution.py:10
  90.2 16.0 %collective-permute-start.2 = (bf16[128,10,128]{2,0,1:T(8,128)(2,1)}, bf16[128,10,128]{2,0,1:T(8,128)(2,1)}, u32[]{:S(2)}, u32[]{:S(2)}) collective-permute-start(bf16[128,10,128]{2,0,1:T(8,128)(2,1)} %fusion.48), channel_id=1, source_target_pairs={{0,1},{1,2},{2,3},{3,0},{4,5},{5,6},{6,7},{7,4},{8,9},{9,10},{10,1... | collective-permute-start | bytes 983048 | tf_op jit(solution)/shard_map/while/body/eval_jaxpr/ppermute | solution.py:10
  109.1 21.0 %collective-permute-start = (bf16[1,128,1280]{1,2,0:T(8,128)(2,1)S(1)}, bf16[1,128,1280]{1,2,0:T(8,128)(2,1)}, u32[]{:S(2)}, u32[]{:S(2)}) collective-permute-start(bf16[1,128,1280]{1,2,0:T(8,128)(2,1)S(1)} %copy.89), channel_id=1, source_target_pairs={{0,1},{1,2},{2,3},{3,0},{4,5},{5,6},{6,7},{7,4},{8,9},{9,10},{10,1... | collective-permute-start | bytes 983048 | tf_op jit(solution)/shard_map/while/body/eval_jaxpr/ppermute | solution.py:10
  109.2 20.9 %collective-permute-start.1 = (bf16[1,128,1280]{1,2,0:T(8,128)(2,1)S(1)}, bf16[1,128,1280]{1,2,0:T(8,128)(2,1)S(1)}, u32[]{:S(2)}, u32[]{:S(2)}) collective-permute-start(bf16[1,128,1280]{1,2,0:T(8,128)(2,1)S(1)} %copy.90), channel_id=1, source_target_pairs={{0,1},{1,2},{2,3},{3,0},{4,5},{5,6},{6,7},{7,4},{8,9},{9,10},{10,1... | collective-permute-start | bytes 983048 | tf_op jit(solution)/shard_map/while/body/eval_jaxpr/ppermute | solution.py:10
  113.1 15.1 %collective-permute-start.2 = (bf16[128,10,128]{2,0,1:T(8,128)(2,1)}, bf16[128,10,128]{2,0,1:T(8,128)(2,1)}, u32[]{:S(2)}, u32[]{:S(2)}) collective-permute-start(bf16[128,10,128]{2,0,1:T(8,128)(2,1)} %fusion.48), channel_id=1, source_target_pairs={{0,1},{1,2},{2,3},{3,0},{4,5},{5,6},{6,7},{7,4},{8,9},{9,10},{10,1... | collective-permute-start | bytes 983048 | tf_op jit(solution)/shard_map/while/body/eval_jaxpr/ppermute | solution.py:10
  144.4 63.6 %copy-start.2 = (f32[128,10,128]{2,0,1:T(8,128)S(1)}, f32[128,10,128]{2,0,1:T(8,128)}, u32[]{:S(2)}) copy-start(f32[128,10,128]{2,0,1:T(8,128)} %get-tuple-element.271) | copy-start | bytes 1966084
  144.4 65.8 %copy-start.1 = (f32[128,10,128]{2,0,1:T(8,128)S(1)}, f32[128,10,128]{2,0,1:T(8,128)}, u32[]{:S(2)}) copy-start(f32[128,10,128]{2,0,1:T(8,128)} %get-tuple-element.272) | copy-start | bytes 1966084
  144.4 90.0 %reduce-scatter.5.cloned.1.call-start = ((), (), s32[]{:S(2)}) async-start(), calls=%async_computation.3 | async-start | bytes 1228800 | tf_op jit(solution)/shard_map/reduce_scatter | solution.py:87
Sparse Core Ops, SparseCore 0:
  144.5 61.2 reduce-scatter.6
  208.1 26.2 reduce-scatter.4
